TPU v7x, 32 devices: a whole 2x2x4 slice. The times are simulated.
32 devices in a mesh: row: 8 (over z, core), col: 4 (over y, x).
Axes of the slice: x: 2, y: 2, z: 4, core: 2. Of those that a mesh axis runs over, the one named last changes fastest.
Arguments:
- shot_traces: float32 [16384, 2, 8192], P(('row', 'col')), may hold values from -0.046875 to 0.046875
- shot_ids: int32 [16384], P(('row', 'col')), may hold values from 0 to 8191, as said below
- shot_counts: int32 [32], P(('row', 'col')), may hold values from 0 to 512, as said below
- missing_blocks: int32 [64, 64], P('row', 'col'), may hold values from 0 to 1, as said below
- weight_bins: int32 [8192], P(('row', 'col')), may hold values from 0 to 63
- weight_table: float32 [64], replicated, may hold values from 0.1 to 1
- focus_panel: float32 [2, 8192, 512], P(None, ('col', 'row')), may hold values from -6 to 6
Outputs:
- wavefield: float32 [2, 8192, 512], P(None, ('row', 'col'))
- adjoint_image: float32 [2, 8192, 512], P(None, ('col', 'row'))
Inputs may be any that keep to these rules, and one draw needn't show every extreme that they name: `shot_ids`: over the counted slots of all devices every source appears exactly once; uncounted slots hold arbitrary sources. The counted slots of one device hold at most 64 sources of any block of 1024 consecutive sources, and at most (128) of any block of 2048; some device reaches both. `shot_counts`: some device has all 512 slots counted. `missing_blocks`: diagonal blocks are recorded, and of two mirrored blocks at most one is missing.
All inputs are finite; a program needn't handle non-finite values.
Results may differ from a plain program's by a relative error of at most 0.00007.
Values sent between devices are 32-bit elements; how exact they have to be, the bound alone decides.
A program may use at most 320 MiB of HBM per device.

v0:
```python
import jax
import jax.numpy as jnp
from jax import lax
from jax.sharding import PartitionSpec as P


def high_dot(left, right):
    return jnp.dot(left, right, precision=lax.Precision.HIGHEST, preferred_element_type=jnp.float32)


def trans_dot(left, right):
    return lax.dot_general(
        left,
        right,
        (((0,), (0,)), ((), ())),
        precision=lax.Precision.HIGHEST,
        preferred_element_type=jnp.float32,
    )


def pack_slots(traces, labels, held_count, group_size, group_count, capacity):
    slot_total = labels.shape[0]
    slot_index = jnp.arange(slot_total, dtype=jnp.int32)
    is_used = slot_index < held_count
    dest_group = labels // group_size
    onehot = (
        (dest_group[:, None] == jnp.arange(group_count, dtype=jnp.int32)[None, :])
        & is_used[:, None]
    ).astype(jnp.int32)
    before = jnp.cumsum(onehot, axis=0) - onehot
    rank_in = jnp.sum(before * onehot, axis=1)
    position = jnp.where(is_used, dest_group * capacity + rank_in, group_count * capacity)
    source = (
        jnp.full((group_count * capacity,), slot_total, jnp.int32)
        .at[position]
        .set(slot_index, mode="drop")
    )
    packed = jnp.take(traces, source, axis=0, mode="fill", fill_value=0.0)
    packed_labels = jnp.take(labels, source, axis=0, mode="fill", fill_value=-1)
    return (packed, packed_labels)


def place_rows(arrived, labels, first_label, length):
    has_label = labels >= 0
    target = jnp.where(has_label, labels - first_label, length)
    source = (
        jnp.zeros((length,), jnp.int32)
        .at[target]
        .set(jnp.arange(labels.shape[0], dtype=jnp.int32), mode="drop")
    )
    return jnp.take(arrived, source, axis=0)


def lookup(bins, table):
    matches = bins[:, None] == jnp.arange(table.shape[0], dtype=jnp.int32)[None, :]
    return jnp.sum(jnp.where(matches, table[None, :], 0.0), axis=1)


def local(
    shot_traces, shot_ids, shot_counts, missing_blocks, weight_bins, weight_table, focus_panel
):
    slot_total = shot_traces.shape[0]
    stations = shot_traces.shape[2]
    row_count = lax.axis_size("row")
    col_count = lax.axis_size("col")
    src_tile = stations // row_count
    rcv_tile = stations // col_count
    row_index = lax.axis_index("row")
    col_index = lax.axis_index("col")
    held_count = shot_counts[0]
    packed, packed_labels = pack_slots(
        shot_traces, shot_ids, held_count, src_tile, row_count, slot_total // row_count
    )
    outgoing = packed.reshape(slot_total, 2, col_count, rcv_tile)
    label_copies = jnp.broadcast_to(packed_labels[:, None, None], (slot_total, 1, col_count))
    arrived, arrived_labels = (
        lax.all_to_all(
            lax.all_to_all(outgoing, "row", split_axis=0, concat_axis=0, tiled=True),
            "col",
            split_axis=2,
            concat_axis=0,
            tiled=True,
        ),
        lax.all_to_all(
            lax.all_to_all(label_copies, "row", split_axis=0, concat_axis=0, tiled=True),
            "col",
            split_axis=2,
            concat_axis=0,
            tiled=True,
        ),
    )
    direct = place_rows(
        arrived.reshape(-1, 2, rcv_tile), arrived_labels.reshape(-1), row_index * src_tile, src_tile
    )
    capacity_rec = slot_total // col_count
    packed_mirror, mirror_labels = pack_slots(
        shot_traces, shot_ids, held_count, rcv_tile, col_count, capacity_rec
    )
    mirror_out = packed_mirror.reshape(slot_total, 2, row_count, src_tile)
    mirror_copies = jnp.broadcast_to(mirror_labels[:, None, None], (slot_total, 1, row_count))
    halfway, halfway_labels = (
        lax.all_to_all(mirror_out, "row", split_axis=2, concat_axis=0, tiled=True),
        lax.all_to_all(mirror_copies, "row", split_axis=2, concat_axis=0, tiled=True),
    )
    halfway = halfway.reshape(row_count, col_count, capacity_rec, 2, src_tile)
    halfway_labels = halfway_labels.reshape(row_count, col_count, capacity_rec)
    mirrored, mirrored_labels = (
        lax.all_to_all(halfway, "col", split_axis=1, concat_axis=0, tiled=True),
        lax.all_to_all(halfway_labels, "col", split_axis=1, concat_axis=0, tiled=True),
    )
    transposed = place_rows(
        mirrored.reshape(-1, 2, src_tile),
        mirrored_labels.reshape(-1),
        col_index * rcv_tile,
        rcv_tile,
    )
    blocks_down = missing_blocks.shape[0]
    blocks_across = missing_blocks.shape[1]
    block_size = src_tile // blocks_down
    is_missing = jnp.broadcast_to(
        missing_blocks[:, None, :, None] > 0, (blocks_down, block_size, blocks_across, block_size)
    ).reshape(src_tile, rcv_tile)
    kernel_re = jnp.where(is_missing, transposed[:, 0, :].T, direct[:, 0, :])
    kernel_im = jnp.where(is_missing, transposed[:, 1, :].T, direct[:, 1, :])
    focus_all = lax.all_gather(focus_panel, "row", axis=1, tiled=True)
    panel_re = focus_all[0]
    panel_im = focus_all[1]
    field_re = high_dot(kernel_re, panel_re) - high_dot(kernel_im, panel_im)
    field_im = high_dot(kernel_re, panel_im) + high_dot(kernel_im, panel_re)
    own_rows = lax.psum_scatter(
        jnp.stack([field_re, field_im], axis=1), "col", scatter_dimension=0, tiled=True
    )
    weighted = own_rows * lookup(weight_bins, weight_table)[:, None, None]
    weighted_all = lax.all_gather(weighted, "col", axis=0, tiled=True)
    weighted_re = weighted_all[:, 0, :]
    weighted_im = weighted_all[:, 1, :]
    image_re = trans_dot(kernel_re, weighted_re) + trans_dot(kernel_im, weighted_im)
    image_im = trans_dot(kernel_re, weighted_im) - trans_dot(kernel_im, weighted_re)
    image_rows = lax.psum_scatter(
        jnp.stack([image_re, image_im], axis=1), "row", scatter_dimension=0, tiled=True
    )
    return (jnp.swapaxes(own_rows, 0, 1), jnp.swapaxes(image_rows, 0, 1))


def solution(mesh):
    placed = (
        P(("row", "col"), None, None),
        P(("row", "col")),
        P(("row", "col")),
        P("row", "col"),
        P(("row", "col")),
        P(),
        P(None, ("col", "row"), None),
    )
    return jax.shard_map(
        local,
        mesh=mesh,
        in_specs=placed,
        out_specs=(P(None, ("row", "col"), None), P(None, ("col", "row"), None)),
        check_vma=False,
    )
```

profile of v0, /device:TPU:0, one launch (start us, length us, event | category | flops | bytes accessed | tf_op | source)
XLA Modules:
  0.0 3004.8 jit_solution(7320027503806781261)
XLA Ops:
  49.6 45.2 %gather_fusion.3 = f32[512,2,8192]{2,1,0:T(2,128)} fusion(f32[512,2,8192]{2,1,0:T(2,128)} %param.11, s32[1024]{0:T(1024)S(1)} %pad_clamp_fusion.1), kind=kCustom, calls=%fused_computation.1.clone | custom fusion | bytes 67110912 | tf_op jit(solution)/shard_map/jit(_take)/gather | solution.py:38
  100.2 24.2 broadcast_select_fusion.1
  124.4 48.8 %copy.56 = f32[512,2,8192]{0,2,1:T(8,128)} copy(f32[512,2,8192]{2,1,0:T(2,128)} %broadcast_select_fusion.1) | data formatting | bytes 67108864 | tf_op jit(solution)/shard_map/jit(_take)/select_n | solution.py:38
  173.1 22.9 copy.57
  203.9 46.5 %gather_fusion.5 = f32[512,2,8192]{2,1,0:T(2,128)} fusion(f32[512,2,8192]{2,1,0:T(2,128)} %param.11, s32[1024]{0:T(1024)S(1)} %pad_clamp_fusion), kind=kCustom, calls=%fused_computation.3.clone | custom fusion | bytes 67110912 | tf_op jit(solution)/shard_map/jit(_take)/gather | solution.py:38
  250.5 24.2 broadcast_select_fusion
  274.6 48.7 %copy.64 = f32[512,2,8192]{0,2,1:T(8,128)} copy(f32[512,2,8192]{2,1,0:T(2,128)} %broadcast_select_fusion) | data formatting | bytes 67108864 | tf_op jit(solution)/shard_map/jit(_take)/select_n | solution.py:38
  323.4 39.8 %copy.65 = f32[512,2,4,2048]{3,2,1,0:T(4,128)} copy(f32[512,2,4,2048]{0,3,2,1:T(8,128)} %bitcast.133) | data formatting | bytes 67108864 | tf_op jit(solution)/shard_map/reshape | solution.py:74
  363.2 563.9 %all-to-all-done.2 = f32[512,2,8,1024]{0,3,1,2:T(8,128)} async-done(((f32[512,2,8,1024]{0,3,1,2:T(8,128)}), f32[512,2,8,1024]{0,3,1,2:T(8,128)}, u32[]{:S(2)}, u32[]{:S(2)}) %all-to-all-start.2) | async-done | bytes 33554464 | tf_op jit(solution)/shard_map/all_to_all | solution.py:102
  934.2 31.9 %copy.58 = f32[512,2,8,1024]{3,0,1,2:T(8,128)} copy(f32[512,2,8,1024]{0,3,1,2:T(8,128)} %all-to-all-done.2) | data formatting | bytes 67108864 | tf_op jit(solution)/shard_map/all_to_all | solution.py:102
  966.1 23.4 copy.59
  989.5 667.9 %all-to-all-done.6 = f32[512,2,4,2048]{3,2,1,0:T(4,128)} async-done(((f32[512,2,4,2048]{3,2,1,0:T(4,128)}), f32[512,2,4,2048]{3,2,1,0:T(4,128)}, u32[]{:S(2)}, u32[]{:S(2)}) %all-to-all-start.6) | async-done | bytes 33554464 | tf_op jit(solution)/shard_map/all_to_all | solution.py:78
  1667.1 37.9 %copy.66 = f32[512,2,4,2048]{0,3,1,2:T(8,128)} copy(f32[512,2,4,2048]{3,2,1,0:T(4,128)} %all-to-all-done.6) | data formatting | bytes 67108864 | tf_op jit(solution)/shard_map/all_to_all | solution.py:78
  1705.0 324.4 %all-to-all-done.3 = f32[8,4,128,2,1024]{4,2,3,0,1:T(8,128)} async-done(((f32[8,4,128,2,1024]{4,2,3,0,1:T(8,128)}), f32[8,4,128,2,1024]{4,2,3,0,1:T(8,128)}, u32[]{:S(2)}, u32[]{:S(2)}) %all-to-all-start.3) | async-done | bytes 33554464 | tf_op jit(solution)/shard_map/all_to_all | solution.py:108
  2048.2 15.9 scatter_custom_fusion.1
  2064.1 23.5 copy.60
  2087.6 55.0 %copy.61 = f32[4096,2,1024]{2,1,0:T(2,128)} copy(f32[4096,2,1024]{2,0,1:T(8,128)} %bitcast.135) | data formatting | bytes 67108864 | tf_op jit(solution)/shard_map/reshape | solution.py:112
  2142.7 258.0 %all-to-all-done.7 = f32[512,2,4,2048]{0,3,1,2:T(8,128)} async-done(((f32[512,2,4,2048]{0,3,1,2:T(8,128)}), f32[512,2,4,2048]{0,3,1,2:T(8,128)}, u32[]{:S(2)}, u32[]{:S(2)}) %all-to-all-start.7) | async-done | bytes 33554464 | tf_op jit(solution)/shard_map/all_to_all | solution.py:77
  2400.6 31.8 %copy.67 = f32[512,2,4,2048]{3,0,2,1:T(8,128)} copy(f32[512,2,4,2048]{0,3,1,2:T(8,128)} %all-to-all-done.7) | data formatting | bytes 67108864 | tf_op jit(solution)/shard_map/all_to_all | solution.py:77
  2432.4 55.0 %copy.68 = f32[2048,2,2048]{2,1,0:T(2,128)} copy(f32[2048,2,2048]{2,0,1:T(8,128)} %bitcast.136) | data formatting | bytes 67108864 | tf_op jit(solution)/shard_map/reshape | solution.py:93
  2487.5 39.4 %gather_fusion.1 = f32[1024,2,2048]{2,1,0:T(2,128)} fusion(f32[2048,2,2048]{2,1,0:T(2,128)} %copy.68, s32[1024]{0:T(1024)S(1)} %fusion.22), kind=kCustom, calls=%fused_computation.5 | custom fusion | bytes 33558528 | tf_op jit(solution)/shard_map/jit(_take)/gather | solution.py:51
  2526.9 25.0 copy.69
  2551.9 54.2 %gather_fusion = f32[2048,2,1024]{2,1,0:T(2,128)} fusion(f32[4096,2,1024]{2,1,0:T(2,128)} %copy.61, s32[2048]{0:T(1024)S(1)} %fusion.19), kind=kCustom, calls=%fused_computation.4 | custom fusion | bytes 33562624 | tf_op jit(solution)/shard_map/jit(_take)/gather | solution.py:51
  2635.7 19.2 fusion.31
  2655.6 17.8 fusion.1
  2673.4 16.7 fusion.3
  2733.9 51.4 %reduce-scatter.3.cloned.1.call-done = f32[256,2,512]{2,0,1:T(8,128)} async-done(((f32[1024,2,512]{2,0,1:T(8,128)}), f32[256,2,512]{2,0,1:T(8,128)}) %reduce-scatter.3.cloned.1.call-update) | async-done | bytes 1048592 | tf_op jit(solution)/shard_map/reduce_scatter | solution.py:130
  2787.7 52.7 %all-gather.5.cloned.1.call-done = f32[1024,2,512]{2,0,1:T(8,128)} async-done(((f32[256,2,512]{2,0,1:T(8,128)}), f32[1024,2,512]{2,0,1:T(8,128)}) %all-gather.5.cloned.1.call-update) | async-done | bytes 4194320 | tf_op jit(solution)/shard_map/all_gather | solution.py:134
  2840.4 17.2 fusion.6
  2857.7 16.0 fusion.7
  2888.8 15.1 subtract_bitcast_fusion
  2908.2 89.7 %reduce-scatter.5.cloned.1.call-done = f32[256,2,512]{2,0,1:T(8,128)} async-done(((f32[2048,2,512]{2,0,1:T(8,128)}), f32[256,2,512]{2,0,1:T(8,128)}) %reduce-scatter.5.cloned.1.call-update) | async-done | bytes 1048592 | tf_op jit(solution)/shard_map/reduce_scatter | solution.py:139
  (114 shorter events, 186.1 us)
Async XLA Ops:
  22.1 12.5 all-to-all-start.4
  35.1 10.7 all-to-all-start
  45.9 49.6 %all-to-all-start.5 = ((s32[512,1,4]{0,1,2:T(1,128)}), s32[512,1,4]{0,1,2:T(1,128)S(1)}, u32[]{:S(2)}, u32[]{:S(2)}) async-start(s32[512,1,4]{0,1,2:T(1,128)} %copy.63), calls=%async_computation.5 | async-start | bytes 16384 | tf_op jit(solution)/shard_map/all_to_all | solution.py:84
  95.5 0.6 copy-start.5
  96.1 100.0 %all-to-all-start.1 = ((s32[8,4,128]{2,0,1:T(8,128)}), s32[8,4,128]{2,0,1:T(8,128)S(1)}, u32[]{:S(2)}, u32[]{:S(2)}) async-start(s32[8,4,128]{2,0,1:T(8,128)} %bitcast.127), calls=%async_computation.1 | async-start | bytes 32768 | tf_op jit(solution)/shard_map/all_to_all | solution.py:109
  196.0 0.6 copy-start.3
  196.6 730.5 %all-to-all-start.2 = ((f32[512,2,8,1024]{0,3,1,2:T(8,128)}), f32[512,2,8,1024]{0,3,1,2:T(8,128)}, u32[]{:S(2)}, u32[]{:S(2)}) async-start(f32[512,2,8,1024]{0,3,1,2:T(8,128)} %copy.57), calls=%async_computation.2 | async-start | bytes 67108864 | tf_op jit(solution)/shard_map/all_to_all | solution.py:102
  927.1 730.3 %all-to-all-start.6 = ((f32[512,2,4,2048]{3,2,1,0:T(4,128)}), f32[512,2,4,2048]{3,2,1,0:T(4,128)}, u32[]{:S(2)}, u32[]{:S(2)}) async-start(f32[512,2,4,2048]{3,2,1,0:T(4,128)} %copy.65), calls=%async_computation.6 | async-start | bytes 67108864 | tf_op jit(solution)/shard_map/all_to_all | solution.py:78
  1657.4 372.0 %all-to-all-start.3 = ((f32[8,4,128,2,1024]{4,2,3,0,1:T(8,128)}), f32[8,4,128,2,1024]{4,2,3,0,1:T(8,128)}, u32[]{:S(2)}, u32[]{:S(2)}) async-start(f32[8,4,128,2,1024]{4,2,3,0,1:T(8,128)} %copy.59), calls=%async_computation.3 | async-start | bytes 67108864 | tf_op jit(solution)/shard_map/all_to_all | solution.py:108
  1705.0 334.9 %copy-start.7 = (s32[8,16]{1,0:T(8,128)S(1)}, s32[8,16]{1,0:T(8,128)}, u32[]{:S(2)}) copy-start(s32[8,16]{1,0:T(8,128)} %param.14) | copy-start | bytes 1540
  1705.0 335.0 %copy-start.6 = (s32[512,1,4]{0,1,2:T(1,128)S(1)}, s32[512,1,4]{0,1,2:T(1,128)}, u32[]{:S(2)}) copy-start(s32[512,1,4]{0,1,2:T(1,128)} %copy-done.5) | copy-start | bytes 24580
  1705.0 343.1 %copy-start.4 = (s32[8,4,128]{2,0,1:T(8,128)S(1)}, s32[8,4,128]{2,0,1:T(8,128)}, u32[]{:S(2)}) copy-start(s32[8,4,128]{2,0,1:T(8,128)} %copy-done.3) | copy-start | bytes 49156
  2029.4 371.3 %all-to-all-start.7 = ((f32[512,2,4,2048]{0,3,1,2:T(8,128)}), f32[512,2,4,2048]{0,3,1,2:T(8,128)}, u32[]{:S(2)}, u32[]{:S(2)}) async-start(f32[512,2,4,2048]{0,3,1,2:T(8,128)} %copy.66), calls=%async_computation.7 | async-start | bytes 67108864 | tf_op jit(solution)/shard_map/all_to_all | solution.py:77
  2039.1 634.3 %all-gather.3.cloned.1.call-start = ((), (), s32[]{:S(2)}) async-start(), calls=%async_computation.10 | async-start | bytes 9437184 | tf_op jit(solution)/shard_map/all_gather | solution.py:125
  2039.8 745.5 %reduce-scatter.3.cloned.1.call-start = ((), (), s32[]{:S(2)}) async-start(), calls=%async_computation.11 | async-start | bytes 5242880 | tf_op jit(solution)/shard_map/reduce_scatter | solution.py:130
  2606.1 16.5 copy-start.1
  2673.4 16.8 copy-start
  2673.4 16.8 copy-start.10
  2690.2 27.4 slice-start.2
  2703.9 13.6 slice-start.3
  2731.3 2.5 copy-start.8
  2731.3 2.5 copy-start.9
  2733.8 106.6 %all-gather.5.cloned.1.call-start = ((), (), s32[]{:S(2)}) async-start(), calls=%async_computation.12 | async-start | bytes 5242880 | tf_op jit(solution)/shard_map/all_gather | solution.py:134
  2787.7 210.2 %reduce-scatter.5.cloned.1.call-start = ((), (), s32[]{:S(2)}) async-start(), calls=%async_computation.13 | async-start | bytes 9437184 | tf_op jit(solution)/shard_map/reduce_scatter | solution.py:139
  2840.4 17.3 copy-start.2
  2840.4 33.3 %slice-start = ((s8[8388608]{0:T(1024)(128)(4,1)}), s8[4194304]{0:T(1024)(128)(4,1)S(1)}, s32[]{:S(2)}) async-start(s8[8388608]{0:T(1024)(128)(4,1)} %bitcast.137), calls=%async_computation.14 | async-start | bytes 8388608
  2857.7 16.0 slice-start.1
Sparse Core Ops, SparseCore 0:
  2041.5 81.8 all-gather.2
  2733.9 51.3 reduce-scatter.2
  2787.8 52.5 all-gather.4
  2908.3 89.5 reduce-scatter.4
where the time goes:
time: 3020 us; the launch traced here: 3000 us
  waiting for transfers between devices  2010 us (67%)
  local copies, waits for them, and re-layouts  696 us (23%)
  matrix products  121 us (4%)
  other arithmetic  106 us (4%)
  starting transfers between devices  53.3 us (2%)
    all_to_all x1, waiting for transfers between devices, local(): lax.all_to_all(outgoing, 'row', split_axis=0, concat_axis=0, tiled=True)  668 us
    all_to_all x1, waiting for transfers between devices, local(): lax.all_to_all(mirror_out, 'row', split_axis=2, concat_axis=0, tiled=True)  564 us
    all_to_all x1, waiting for transfers between devices, local(): lax.all_to_all(halfway, 'col', split_axis=1, concat_axis=0, tiled=True)  324 us
    all_to_all x1, waiting for transfers between devices, local(): lax.all_to_all(lax.all_to_all(outgoing, 'row', split_axis=0, concat_axis=...  258 us
    gather x3, local copies, waits for them, and re-layouts, place_rows(): return jnp.take(arrived, source, axis=0)  119 us
    select_n x2, local copies, waits for them, and re-layouts, pack_slots(): packed = jnp.take(traces, source, axis=0, mode='fill', fill_value=0.0)  97.5 us
    gather x2, local copies, waits for them, and re-layouts, pack_slots(): packed = jnp.take(traces, source, axis=0, mode='fill', fill_value=0.0)  91.8 us
    reduce_scatter x1, waiting for transfers between devices, local(): lax.psum_scatter(jnp.stack([image_re, image_im], axis=1), 'row', scatter_...  89.7 us
  transfers between devices with their start and end apart: 12, of which 8 were waited for; matrix products, arithmetic and copies ran while one was open for 26% of the time, Pallas kernels for 0%

commit v1 on v0

--- a/solution.py
+++ b/solution.py
@@ -2,6 +2,13 @@
 import jax.numpy as jnp
 from jax import lax
 from jax.sharding import PartitionSpec as P
+
+
+def swap_blocks(block, axis, split, join):
+    size = lax.axis_size(axis)
+    parts = jnp.stack(jnp.split(block, size, axis=split), axis=0)
+    parts = lax.all_to_all(parts, axis, split_axis=0, concat_axis=0)
+    return jnp.concatenate(parts, axis=join)
 
 
 def high_dot(left, right):
@@ -74,12 +81,8 @@
     outgoing = packed.reshape(slot_total, 2, col_count, rcv_tile)
     label_copies = jnp.broadcast_to(packed_labels[:, None, None], (slot_total, 1, col_count))
     arrived, arrived_labels = (
-        lax.all_to_all(
-            lax.all_to_all(outgoing, "row", split_axis=0, concat_axis=0, tiled=True),
-            "col",
-            split_axis=2,
-            concat_axis=0,
-            tiled=True,
+        swap_blocks(
+            lax.all_to_all(outgoing, "row", split_axis=0, concat_axis=0, tiled=True), "col", 2, 0
         ),
         lax.all_to_all(
             lax.all_to_all(label_copies, "row", split_axis=0, concat_axis=0, tiled=True),

time: 3020 us -> 2930 us (0.970)
  local copies, waits for them, and re-layouts: 696 us -> 506 us
  waiting for transfers between devices: 2010 us -> 2100 us
    reshape x2 -> x0, local copies, waits for them, and re-layouts: 94.8 us -> none  [the longest x1 55 us: local(): arrived.reshape(-1, 2, rcv_tile)]
    all_to_all x1, waiting for transfers between devices: 564 us -> 652 us  [local(): lax.all_to_all(mirror_out, 'row', split_axis=2, concat_axis=0, tiled=True)]
    all_to_all x2 -> x0, local copies, waits for them, and re-layouts: 69.7 us -> none  [the longest x1 37.9 us: local(): lax.all_to_all(outgoing, 'row', split_axis=0, concat_axis=0, tiled=True)]
    select_n x2 -> x1, local copies, waits for them, and re-layouts: 97.5 us -> 48.7 us  [pack_slots(): packed = jnp.take(traces, source, axis=0, mode='fill', fill_value=0.0)]
  transfers between devices with their start and end apart: 12 -> 12, of which waited for: 8 -> 8; matrix products, arithmetic and copies ran while one was open for 26% -> 21% of each run, Pallas kernels for 0% -> 0%
where the time goes in v1:
time: 2930 us; the launch traced here: 2920 us
  waiting for transfers between devices  2100 us (72%)
  local copies, waits for them, and re-layouts  506 us (17%)
  other arithmetic  127 us (4%)
  matrix products  121 us (4%)
  starting transfers between devices  53.4 us (2%)
    all_to_all x1, waiting for transfers between devices, local(): lax.all_to_all(outgoing, 'row', split_axis=0, concat_axis=0, tiled=True)  668 us
    all_to_all x1, waiting for transfers between devices, local(): lax.all_to_all(mirror_out, 'row', split_axis=2, concat_axis=0, tiled=True)  652 us
    all_to_all x1, waiting for transfers between devices, local(): lax.all_to_all(halfway, 'col', split_axis=1, concat_axis=0, tiled=True)  319 us
    all_to_all x1, waiting for transfers between devices, swap_blocks(): parts = lax.all_to_all(parts, axis, split_axis=0, concat_axis=0)  258 us
    gather x3, local copies, waits for them, and re-layouts, place_rows(): return jnp.take(arrived, source, axis=0)  119 us
    gather x2, local copies, waits for them, and re-layouts, pack_slots(): packed = jnp.take(traces, source, axis=0, mode='fill', fill_value=0.0)  91.8 us
    reduce_scatter x1, waiting for transfers between devices, local(): lax.psum_scatter(jnp.stack([image_re, image_im], axis=1), 'row', scatter_...  89.7 us
    dot_general x4, matrix products, trans_dot(): lax.dot_general(left, right, (((0,), (0,)), ((), ())), precision=lax.Prec...  63.5 us
  transfers between devices with their start and end apart: 12, of which 8 were waited for; matrix products, arithmetic and copies ran while one was open for 21% of the time, Pallas kernels for 0%

profile of v1, /device:TPU:0, one launch (start us, length us, event | category | flops | bytes accessed | tf_op | source)
XLA Modules:
  0.0 2918.0 jit_solution(6057759850904522265)
XLA Ops:
  49.6 45.2 %gather_fusion.3 = f32[512,2,8192]{2,1,0:T(2,128)} fusion(f32[512,2,8192]{2,1,0:T(2,128)} %param.11, s32[1024]{0:T(1024)S(1)} %pad_clamp_fusion.1), kind=kCustom, calls=%fused_computation.1.clone | custom fusion | bytes 67110912 | tf_op jit(solution)/shard_map/jit(_take)/gather | solution.py:45
  100.2 24.2 broadcast_select_fusion.1
  124.4 48.7 %copy.57 = f32[512,2,8192]{0,2,1:T(8,128)} copy(f32[512,2,8192]{2,1,0:T(2,128)} %broadcast_select_fusion.1) | data formatting | bytes 67108864 | tf_op jit(solution)/shard_map/jit(_take)/select_n | solution.py:45
  173.1 22.9 copy.58
  203.9 46.5 %gather_fusion.5 = f32[512,2,8192]{2,1,0:T(2,128)} fusion(f32[512,2,8192]{2,1,0:T(2,128)} %param.11, s32[1024]{0:T(1024)S(1)} %pad_clamp_fusion), kind=kCustom, calls=%fused_computation.3.clone | custom fusion | bytes 67110912 | tf_op jit(solution)/shard_map/jit(_take)/gather | solution.py:45
  250.4 24.2 broadcast_select_fusion
  274.6 652.4 %all-to-all-done.2 = f32[512,2,8,1024]{0,3,1,2:T(8,128)} async-done(((f32[512,2,8,1024]{0,3,1,2:T(8,128)}), f32[512,2,8,1024]{0,3,1,2:T(8,128)}, u32[]{:S(2)}, u32[]{:S(2)}) %all-to-all-start.2) | async-done | bytes 33554464 | tf_op jit(solution)/shard_map/all_to_all | solution.py:105
  934.2 31.8 %copy.59 = f32[512,2,8,1024]{3,0,1,2:T(8,128)} copy(f32[512,2,8,1024]{0,3,1,2:T(8,128)} %all-to-all-done.2) | data formatting | bytes 67108864 | tf_op jit(solution)/shard_map/all_to_all | solution.py:105
  966.1 23.4 copy.60
  989.5 667.9 %all-to-all-done.6 = f32[512,2,4,2048]{3,1,2,0:T(2,128)} async-done(((f32[512,2,4,2048]{3,1,2,0:T(2,128)}), f32[512,2,4,2048]{3,1,2,0:T(2,128)}, u32[]{:S(2)}, u32[]{:S(2)}) %all-to-all-start.6) | async-done | bytes 33554464 | tf_op jit(solution)/shard_map/all_to_all | solution.py:85
  1667.1 22.8 slice_bitcast_fusion.5
  1689.9 20.1 pad_maximum_fusion
  1710.0 319.3 %all-to-all-done.3 = f32[8,4,128,2,1024]{4,2,3,0,1:T(8,128)} async-done(((f32[8,4,128,2,1024]{4,2,3,0,1:T(8,128)}), f32[8,4,128,2,1024]{4,2,3,0,1:T(8,128)}, u32[]{:S(2)}, u32[]{:S(2)}) %all-to-all-start.3) | async-done | bytes 33554464 | tf_op jit(solution)/shard_map/all_to_all | solution.py:111
  2048.2 15.9 scatter_custom_fusion.1
  2064.1 23.5 copy.61
  2087.6 55.0 %copy.62 = f32[4096,2,1024]{2,1,0:T(2,128)} copy(f32[4096,2,1024]{2,0,1:T(8,128)} %bitcast.145) | data formatting | bytes 67108864 | tf_op jit(solution)/shard_map/reshape | solution.py:115
  2142.7 258.0 %all-to-all-done.7 = f32[4,512,2,1,2048]{4,2,1,3,0:T(2,128)} async-done(((f32[4,512,2,1,2048]{4,2,1,3,0:T(2,128)}), f32[4,512,2,1,2048]{4,2,1,3,0:T(2,128)}, u32[]{:S(2)}, u32[]{:S(2)}) %all-to-all-start.7) | async-done | bytes 33554464 | tf_op jit(solution)/shard_map/all_to_all | solution.py:10
  2400.7 39.4 %gather_fusion.1 = f32[1024,2,2048]{2,1,0:T(2,128)} fusion(f32[2048,2,2048]{2,1,0:T(2,128)} %bitcast.34, s32[1024]{0:T(1024)S(1)} %fusion.22), kind=kCustom, calls=%fused_computation.5 | custom fusion | bytes 33558528 | tf_op jit(solution)/shard_map/jit(_take)/gather | solution.py:58
  2440.1 25.0 copy.68
  2465.1 54.2 %gather_fusion = f32[2048,2,1024]{2,1,0:T(2,128)} fusion(f32[4096,2,1024]{2,1,0:T(2,128)} %copy.62, s32[2048]{0:T(1024)S(1)} %fusion.19), kind=kCustom, calls=%fused_computation.4 | custom fusion | bytes 33562624 | tf_op jit(solution)/shard_map/jit(_take)/gather | solution.py:58
  2548.9 19.2 fusion.31
  2568.7 17.8 fusion.1
  2586.6 16.7 fusion.3
  2603.3 13.8 fusion.2
  2630.7 13.8 add_bitcast_fusion.1
  2647.1 51.4 %reduce-scatter.3.cloned.1.call-done = f32[256,2,512]{2,0,1:T(8,128)} async-done(((f32[1024,2,512]{2,0,1:T(8,128)}), f32[256,2,512]{2,0,1:T(8,128)}) %reduce-scatter.3.cloned.1.call-update) | async-done | bytes 1048592 | tf_op jit(solution)/shard_map/reduce_scatter | solution.py:133
  2700.9 52.7 %all-gather.5.cloned.1.call-done = f32[1024,2,512]{2,0,1:T(8,128)} async-done(((f32[256,2,512]{2,0,1:T(8,128)}), f32[1024,2,512]{2,0,1:T(8,128)}) %all-gather.5.cloned.1.call-update) | async-done | bytes 4194320 | tf_op jit(solution)/shard_map/all_gather | solution.py:137
  2753.5 17.2 fusion.6
  2770.8 16.0 fusion.7
  2786.8 15.1 add_bitcast_fusion
  2801.9 15.1 subtract_bitcast_fusion
  2821.3 89.7 %reduce-scatter.5.cloned.1.call-done = f32[256,2,512]{2,0,1:T(8,128)} async-done(((f32[2048,2,512]{2,0,1:T(8,128)}), f32[256,2,512]{2,0,1:T(8,128)}) %reduce-scatter.5.cloned.1.call-update) | async-done | bytes 1048592 | tf_op jit(solution)/shard_map/reduce_scatter | solution.py:142
  (111 shorter events, 143.5 us)
Async XLA Ops:
  22.1 12.5 all-to-all-start.4
  35.1 10.7 all-to-all-start
  45.9 49.6 %all-to-all-start.5 = ((s32[512,1,4]{0,1,2:T(1,128)}), s32[512,1,4]{0,1,2:T(1,128)S(1)}, u32[]{:S(2)}, u32[]{:S(2)}) async-start(s32[512,1,4]{0,1,2:T(1,128)} %copy.64), calls=%async_computation.5 | async-start | bytes 16384 | tf_op jit(solution)/shard_map/all_to_all | solution.py:87
  95.5 0.6 copy-start.5
  96.1 99.9 %all-to-all-start.1 = ((s32[8,4,128]{2,0,1:T(8,128)}), s32[8,4,128]{2,0,1:T(8,128)S(1)}, u32[]{:S(2)}, u32[]{:S(2)}) async-start(s32[8,4,128]{2,0,1:T(8,128)} %bitcast.137), calls=%async_computation.1 | async-start | bytes 32768 | tf_op jit(solution)/shard_map/all_to_all | solution.py:112
  196.0 0.6 copy-start.3
  196.6 730.5 %all-to-all-start.2 = ((f32[512,2,8,1024]{0,3,1,2:T(8,128)}), f32[512,2,8,1024]{0,3,1,2:T(8,128)}, u32[]{:S(2)}, u32[]{:S(2)}) async-start(f32[512,2,8,1024]{0,3,1,2:T(8,128)} %copy.58), calls=%async_computation.2 | async-start | bytes 67108864 | tf_op jit(solution)/shard_map/all_to_all | solution.py:105
  927.0 730.4 %all-to-all-start.6 = ((f32[512,2,4,2048]{3,1,2,0:T(2,128)}), f32[512,2,4,2048]{3,1,2,0:T(2,128)}, u32[]{:S(2)}, u32[]{:S(2)}) async-start(f32[512,2,4,2048]{3,1,2,0:T(2,128)} %bitcast.142), calls=%async_computation.6 | async-start | bytes 67108864 | tf_op jit(solution)/shard_map/all_to_all | solution.py:85
  1657.4 372.0 %all-to-all-start.3 = ((f32[8,4,128,2,1024]{4,2,3,0,1:T(8,128)}), f32[8,4,128,2,1024]{4,2,3,0,1:T(8,128)}, u32[]{:S(2)}, u32[]{:S(2)}) async-start(f32[8,4,128,2,1024]{4,2,3,0,1:T(8,128)} %copy.60), calls=%async_computation.3 | async-start | bytes 67108864 | tf_op jit(solution)/shard_map/all_to_all | solution.py:111
  1710.0 329.9 %copy-start.7 = (s32[8,16]{1,0:T(8,128)S(1)}, s32[8,16]{1,0:T(8,128)}, u32[]{:S(2)}) copy-start(s32[8,16]{1,0:T(8,128)} %param.14) | copy-start | bytes 1540
  1710.0 330.0 %copy-start.6 = (s32[512,1,4]{0,1,2:T(1,128)S(1)}, s32[512,1,4]{0,1,2:T(1,128)}, u32[]{:S(2)}) copy-start(s32[512,1,4]{0,1,2:T(1,128)} %copy-done.5) | copy-start | bytes 24580
  1710.0 338.1 %copy-start.4 = (s32[8,4,128]{2,0,1:T(8,128)S(1)}, s32[8,4,128]{2,0,1:T(8,128)}, u32[]{:S(2)}) copy-start(s32[8,4,128]{2,0,1:T(8,128)} %copy-done.3) | copy-start | bytes 49156
  2029.4 371.3 %all-to-all-start.7 = ((f32[4,512,2,1,2048]{4,2,1,3,0:T(2,128)}), f32[4,512,2,1,2048]{4,2,1,3,0:T(2,128)}, u32[]{:S(2)}, u32[]{:S(2)}) async-start(f32[4,512,2,1,2048]{4,2,1,3,0:T(2,128)} %pad_maximum_fusion), calls=%async_computation.7 | async-start | bytes 67108864 | tf_op jit(solution)/shard_map/all_to_all | solution.py:10
  2039.1 547.5 %all-gather.3.cloned.1.call-start = ((), (), s32[]{:S(2)}) async-start(), calls=%async_computation.10 | async-start | bytes 9437184 | tf_op jit(solution)/shard_map/all_gather | solution.py:128
  2039.8 658.6 %reduce-scatter.3.cloned.1.call-start = ((), (), s32[]{:S(2)}) async-start(), calls=%async_computation.11 | async-start | bytes 5242880 | tf_op jit(solution)/shard_map/reduce_scatter | solution.py:133
  2519.3 16.5 copy-start.1
  2586.6 16.7 copy-start
  2586.6 16.8 copy-start.10
  2603.3 27.3 slice-start.2
  2617.1 13.6 slice-start.3
  2644.5 2.5 copy-start.8
  2644.5 2.5 copy-start.9
  2646.9 106.6 %all-gather.5.cloned.1.call-start = ((), (), s32[]{:S(2)}) async-start(), calls=%async_computation.12 | async-start | bytes 5242880 | tf_op jit(solution)/shard_map/all_gather | solution.py:137
  2700.8 210.2 %reduce-scatter.5.cloned.1.call-start = ((), (), s32[]{:S(2)}) async-start(), calls=%async_computation.13 | async-start | bytes 9437184 | tf_op jit(solution)/shard_map/reduce_scatter | solution.py:142
  2753.5 17.2 copy-start.2
  2753.5 33.2 %slice-start = ((s8[8388608]{0:T(1024)(128)(4,1)}), s8[4194304]{0:T(1024)(128)(4,1)S(1)}, s32[]{:S(2)}) async-start(s8[8388608]{0:T(1024)(128)(4,1)} %bitcast.146), calls=%async_computation.14 | async-start | bytes 8388608
  2770.8 16.0 slice-start.1
Sparse Core Ops, SparseCore 0:
  2041.5 81.8 all-gather.2
  2647.0 51.3 reduce-scatter.2
  2700.9 52.5 all-gather.4
  2821.4 89.5 reduce-scatter.4
